TPU v7x, 256 devices: a whole 4x4x8 slice. The times are simulated.
256 devices in a mesh: group: 8 (over z_hi, core), tensor: 8 (over y, z_lo), seq: 4 (over x).
Axes of the slice: x: 4, y: 4, z: 8 (z_hi: 4, z_lo: 2; z = z_hi * 2 + z_lo), core: 2. Of those that a mesh axis runs over, the one named last changes fastest.
Arguments:
- patches: bfloat16 [8192, 1280], P(('group', 'tensor', 'seq')), may hold values from -6 to 6
- enc_gain: float32 [1280], replicated, may hold values from 0.1 to 1.9
- enc_qkv: bfloat16 [3, 1280, 1280], P(None, None, 'tensor')
- enc_out: bfloat16 [1280, 1280], P('tensor'), may hold values from -0.15625 to 0.15625
- cross_kv: bfloat16 [1280, 2048], P(None, 'tensor'), may hold values from -0.15625 to 0.15625
- key_gain: float32 [128], replicated, may hold values from 0.1 to 1.9
- dec_hidden: bfloat16 [4096, 8192], P(('group', 'seq')), may hold values from -6 to 6
- dec_gain: float32 [8192], replicated, may hold values from 0.1 to 1.9
- query_weight: bfloat16 [8192, 4096], P(None, 'tensor'), may hold values from -0.0625 to 0.0625
- query_gain: float32 [128], replicated, may hold values from 1.5 to 3
- image_of_row: int32 [4096], P(('group', 'seq')), may hold values from 0 to 3
- valid_count: int32 [4096], P(('group', 'seq')), may hold values from 1 to 2048, as said below
Outputs:
- decoded: bfloat16 [4096, 4096], P(('group', 'seq'), 'tensor')
Inputs may be any that keep to these rules, and one draw needn't show every extreme that they name: `valid_count`: every draw has a row reading a whole image and a row reading one patch.
All inputs are finite; a program needn't handle non-finite values.
Results may differ from a plain program's by a relative error of at most 0.028.
The roundings to bfloat16 on the way count: a program that leaves them out, or rounds other values in their place, can miss the bound.
Values may be sent and summed in bfloat16 or wider, within the bound.
No kernel may reach another device: no remote copies, remote signals or barrier semaphores. Data moves between devices by JAX's collectives and lax.ppermute only.
A program may use at most 128 MiB of HBM per device.

v0:
```python
import math
import jax
import jax.numpy as jnp
from jax import lax
from jax.sharding import PartitionSpec as P

EHD = 80
HD = 128
IMAGES = 4
EPSILON = 1e-05


def layer_norm(values, gain_vector):
    mean_value = jnp.mean(values, axis=-1, keepdims=True)
    centered = values - mean_value
    variance = jnp.mean(centered * centered, axis=-1, keepdims=True)
    return centered * lax.rsqrt(variance + EPSILON) * gain_vector


def rms_norm(values, gain_vector):
    square_mean = jnp.mean(values * values, axis=-1, keepdims=True)
    return values * lax.rsqrt(square_mean + EPSILON) * gain_vector


def on_device(
    patches,
    enc_gain,
    enc_qkv,
    enc_out,
    cross_kv,
    key_gain,
    dec_hidden,
    dec_gain,
    query_weight,
    query_gain,
    image_of_row,
    valid_count,
):
    tensor_count = lax.axis_size("tensor")
    seq_count = lax.axis_size("seq")
    patch_rows = patches.shape[0]
    deal_block = patch_rows * seq_count
    gathered = lax.all_gather(patches, "tensor", axis=0, tiled=True)
    row_count = gathered.shape[0]
    normed = layer_norm(gathered.astype(jnp.float32), enc_gain).astype(jnp.bfloat16)
    local_width = enc_qkv.shape[2]
    local_heads = local_width // EHD
    query_part = (
        jnp.dot(normed, enc_qkv[0], preferred_element_type=jnp.float32)
        .astype(jnp.bfloat16)
        .reshape(row_count, local_heads, EHD)
    )
    key_part = jnp.dot(normed, enc_qkv[1], preferred_element_type=jnp.float32).astype(jnp.bfloat16)
    value_part = jnp.dot(normed, enc_qkv[2], preferred_element_type=jnp.float32).astype(
        jnp.bfloat16
    )

    def patch_number(gathered_index):
        shard_number = gathered_index // row_count
        within = gathered_index % row_count
        source_tensor = within // patch_rows
        source_row = within % patch_rows
        source_group = shard_number // seq_count
        source_seq = shard_number % seq_count
        return (
            (source_group * tensor_count + source_tensor) * seq_count + source_seq
        ) * patch_rows + source_row

    def image_number(patch_index):
        return patch_index // deal_block % IMAGES

    own_index = jnp.arange(row_count, dtype=jnp.int32)
    own_shard = lax.axis_index("group") * seq_count + lax.axis_index("seq")
    query_image = image_number(patch_number(own_shard * row_count + own_index))
    running_max = jnp.full((local_heads, row_count), -1e30, jnp.float32)
    key_shard = lax.all_gather(key_part, ("group", "seq"), axis=0, tiled=True)
    value_shard = lax.all_gather(value_part, ("group", "seq"), axis=0, tiled=True)
    piece_rows = key_shard.shape[0]
    key_index = jnp.arange(piece_rows, dtype=jnp.int32)
    key_image = image_number(patch_number(key_index))
    same_image = (query_image[:, None] == key_image[None, :])[None]
    key_heads = key_shard.reshape(piece_rows, local_heads, EHD)
    value_heads = value_shard.reshape(piece_rows, local_heads, EHD)
    scores = jnp.einsum(
        "rhd,khd->hrk", query_part, key_heads, preferred_element_type=jnp.float32
    ) / math.sqrt(EHD)
    masked = jnp.where(same_image, scores, jnp.full_like(scores, -1e30))
    new_max = jnp.maximum(running_max, jnp.max(masked, axis=-1))
    weights = jnp.where(same_image, jnp.exp(scores - new_max[..., None]), jnp.zeros_like(scores))
    new_sum = jnp.sum(weights, axis=-1)
    new_mix = jnp.einsum(
        "hrk,khd->hrd",
        weights.astype(jnp.bfloat16),
        value_heads,
        preferred_element_type=jnp.float32,
    )
    folded = (new_max, new_sum, new_mix)
    final_max, final_sum, final_mix = folded
    attended = (final_mix / final_sum[..., None]).astype(jnp.bfloat16)
    attended = attended.transpose(1, 0, 2).reshape(row_count, local_width)
    total_out = lax.psum(
        jnp.dot(attended, enc_out, preferred_element_type=jnp.float32).astype(jnp.bfloat16),
        "tensor",
    ).astype(jnp.float32)
    encoded = (gathered.astype(jnp.float32) + total_out).astype(jnp.bfloat16)
    kv_local = cross_kv.shape[1] // (2 * HD)
    cross_proj = jnp.dot(encoded, cross_kv, preferred_element_type=jnp.float32).reshape(
        row_count, kv_local, 2, HD
    )
    cross_keys = rms_norm(cross_proj[:, :, 0], key_gain)
    kv_slab = (
        jnp.stack([cross_keys, cross_proj[:, :, 1]], axis=2)
        .astype(jnp.bfloat16)
        .reshape(row_count, kv_local * 2 * HD)
    )
    every_slab = lax.all_gather(kv_slab, ("group", "seq"), axis=0, tiled=True)
    dec_rows = dec_hidden.shape[0]
    dec_normed = rms_norm(dec_hidden.astype(jnp.float32), dec_gain).astype(jnp.bfloat16)
    query_local = query_weight.shape[1] // HD
    group_size = query_local // kv_local
    queries = jnp.dot(dec_normed, query_weight, preferred_element_type=jnp.float32).reshape(
        dec_rows, query_local, HD
    )
    queries = (rms_norm(queries, query_gain) / math.sqrt(HD)).astype(jnp.bfloat16)
    queries = queries.reshape(dec_rows, kv_local, group_size, HD)
    slab_rows = every_slab.shape[0]
    slab_view = every_slab.reshape(slab_rows, kv_local, 2, HD)
    patch_index = patch_number(jnp.arange(slab_rows, dtype=jnp.int32))
    slab_image = image_number(patch_index)
    slab_position = patch_index // (deal_block * IMAGES) * deal_block + patch_index % deal_block
    allowed = (slab_image[None, :] == image_of_row[:, None]) & (
        slab_position[None, :] < valid_count[:, None]
    )
    scores = jnp.einsum(
        "rgqd,kgd->gqrk", queries, slab_view[:, :, 0], preferred_element_type=jnp.float32
    )
    weights = jnp.where(allowed[None, None], jnp.exp(scores), jnp.zeros_like(scores))
    weight_sum = jnp.sum(weights, axis=-1)
    mixture = jnp.einsum(
        "gqrk,kgd->rgqd",
        weights.astype(jnp.bfloat16),
        slab_view[:, :, 1],
        preferred_element_type=jnp.float32,
    )
    result = mixture / weight_sum.transpose(2, 0, 1)[..., None]
    return result.astype(jnp.bfloat16).reshape(dec_rows, query_local * HD)


def solution(mesh):
    in_specs = (
        P(("group", "tensor", "seq"), None),
        P(),
        P(None, None, "tensor"),
        P("tensor", None),
        P(None, "tensor"),
        P(),
        P(("group", "seq"), None),
        P(),
        P(None, "tensor"),
        P(),
        P(("group", "seq")),
        P(("group", "seq")),
    )
    out_specs = P(("group", "seq"), "tensor")
    return jax.shard_map(
        on_device, mesh=mesh, in_specs=in_specs, out_specs=out_specs, check_vma=False
    )
```

profile of v0, /device:TPU:1, one launch (start us, length us, event | category | flops | bytes accessed | tf_op | source)
XLA Modules:
  0.0 340.4 jit_solution(16745044006763906302)
XLA Ops:
  6.5 26.6 %all_gather.12 = bf16[256,1280]{1,0:T(8,128)(2,1)S(1)} all-gather(bf16[32,1280]{1,0:T(8,128)(2,1)} %param.12), channel_id=1, replica_groups=mesh['group'=8,'tensor'=8,'seq'=4] {'tensor'}, dimensions={0}, use_global_device_ids=true | all-gather | bytes 737280 | tf_op jit(solution)/shard_map/all_gather | solution.py:43
  33.3 0.3 fusion.22
  33.6 1.0 fusion.24
  34.6 2.0 convolution_convert_fusion.2
  36.7 1.0 convolution_convert_fusion.1
  37.9 0.4 convolution_convert_fusion.3
  38.3 1.2 broadcast_compare_fusion
  39.5 62.9 %all-gather.4.cloned.1.call-done = bf16[8192,160]{0,1:T(8,128)(2,1)} async-done(((bf16[256,160]{0,1:T(8,128)(2,1)}), bf16[8192,160]{0,1:T(8,128)(2,1)}) %all-gather.4.cloned.1.call-update) | async-done | bytes 2621456 | tf_op jit(solution)/shard_map/all_gather | solution.py:76
  102.4 5.6 %select_reduce_fusion = (f32[2,256]{1,0:T(2,128)S(1)}, f32[2,256,8192]{2,1,0:T(8,128)S(1)}) fusion(pred[256,8192]{1,0:T(8,128)(4,1)S(1)} %broadcast_compare_fusion, bf16[256,2,80]{0,2,1:T(8,128)(2,1)S(1)} %bitcast.128, bf16[8192,2,80]{0,2,1:T(8,128)(2,1)} %bitcast.126), kind=kOutput, calls=%fused_computation.2 | convolution fusion | flops 683671040 | bytes 21579776 | tf_op jit(solution)/shard_map/rhd,khd->hrk/dot_general | solution.py:84
  108.0 5.7 %copy-done.1 = f32[2,256,8192]{2,1,0:T(8,128)} copy-done((f32[2,256,8192]{2,1,0:T(8,128)}, f32[2,256,8192]{2,1,0:T(8,128)S(1)}, u32[]{:S(2)}) %copy-start.1) | copy-done | bytes 16777240
  113.7 4.8 %fusion.2 = f32[2,256]{1,0:T(2,128)S(1)} fusion(f32[2,256,8192]{2,1,0:T(8,128)S(1)} %get-tuple-element.6, f32[2,256]{1,0:T(2,128)S(1)} %broadcast_maximum_fusion, pred[256,8192]{1,0:T(8,128)(4,1)S(1)} %broadcast_compare_fusion), kind=kLoop, calls=%fused_computation.5 | loop fusion | flops 16776704 | bytes 18878464 | tf_op jit(solution)/shard_map/reduce_sum | solution.py:90
  118.5 41.9 %all-gather.6.cloned.1.call-done = bf16[8192,160]{0,1:T(8,128)(2,1)} async-done(((bf16[256,160]{0,1:T(8,128)(2,1)}), bf16[8192,160]{0,1:T(8,128)(2,1)}) %all-gather.6.cloned.1.call-update) | async-done | bytes 2621456 | tf_op jit(solution)/shard_map/all_gather | solution.py:77
  160.4 8.5 %fusion.35 = bf16[256,2,80]{0,2,1:T(8,128)(2,1)S(1)} fusion(bf16[8192,2,80]{0,2,1:T(8,128)(2,1)} %bitcast.127, f32[2,256,8192]{2,1,0:T(8,128)} %copy-done.1, f32[2,256]{1,0:T(2,128)S(1)} %broadcast_maximum_fusion, pred[256,8192]{1,0:T(8,128)(4,1)S(1)} %broadcast_compare_fusion, f32[256,2]{0,1:T(2,128)S(1)} %bitcast.123), kind=kOutput, calls=%fused_computation.42 | convolution fusion | flops 687947776 | bytes 21581824 | tf_op jit(solution)/shard_map/hrk,khd->hrd/dot_general | solution.py:91
  169.0 1.2 convolution_convert_fusion
  170.4 74.0 %all-reduce.2.cloned.1.call-done = bf16[256,1280]{1,0:T(8,128)(2,1)} async-done(((bf16[256,1280]{1,0:T(8,128)(2,1)}), bf16[256,1280]{1,0:T(8,128)(2,1)}) %all-reduce.2.cloned.1.call-update) | async-done | bytes 655376 | tf_op jit(solution)/shard_map/psum | solution.py:101
  244.4 1.5 fusion.44
  246.1 0.7 pad_maximum_fusion
  246.8 0.5 fusion.12
  247.4 5.4 %fusion.100 = (f32[128,512]{1,0:T(8,128)S(1)}, f32[128,512]{1,0:T(8,128)}) fusion(bf16[8192,512]{1,0:T(8,128)(2,1)} %param.20, bf16[128,8192]{1,0:T(8,128)(2,1)S(1)} %copy-done.2, f32[8192]{0:T(1024)S(1)} %copy-done.10, f32[128]{0:T(128)S(1)} %add_rsqrt_fusion.3), kind=kOutput, calls=%fused_computation.160 | convolution fusion | flops 1078001664 | bytes 11043328 | tf_op jit(solution)/shard_map/dot_general | solution.py:121
  253.2 2.8 compare_and_fusion
  256.0 58.9 %all-gather.8.cloned.1.call-done = bf16[8192,256]{0,1:T(8,128)(2,1)} async-done(((bf16[256,256]{0,1:T(8,128)(2,1)}), bf16[8192,256]{0,1:T(8,128)(2,1)}) %all-gather.8.cloned.1.call-update) | async-done | bytes 4194320 | tf_op jit(solution)/shard_map/all_gather | solution.py:116
  315.1 10.6 %fusion = (f32[4,128]{1,0:T(4,128)S(1)}, f32[8192,128,4]{1,0,2:T(8,128)}) fusion(pred[128,8192]{0,1:T(8,128)(4,1)S(1)} %compare_and_fusion, bf16[8192,1,2,128]{0,3,2,1:T(8,128)(2,1)} %bitcast.124, f32[128,512]{1,0:T(8,128)} %get-tuple-element.8, f32[16,8,4,128]{3,2,1,0:T(4,128)S(1)} %bitcast.120, f32[512]{0:T(512)S(1)} %broadcast_bitcast_fusion), kind=kOutput, calls=%fused_computation.3 | convolution fusion | flops 1082392064 | bytes 20451328 | tf_op jit(solution)/shard_map/rgqd,kgd->gqrk/dot_general | solution.py:134
  325.7 7.4 %fusion.41 = bf16[128,1,4,128]{0,3,2,1:T(8,128)(2,1)S(1)} fusion(f32[8192,128,4]{1,0,2:T(8,128)} %get-tuple-element.10, pred[128,8192]{0,1:T(8,128)(4,1)S(1)} %compare_and_fusion, bf16[8192,1,2,128]{0,3,2,1:T(8,128)(2,1)S(1)} %bitcast.125, f32[128,4]{0,1:T(4,128)S(1)} %bitcast.129), kind=kOutput, calls=%fused_computation.44 | convolution fusion | flops 1082261504 | bytes 20056064 | tf_op jit(solution)/shard_map/gqrk,kgd->rgqd/dot_general | solution.py:139
  333.1 0.8 copy.31
  (46 shorter events, 1.4 us)
Async XLA Ops:
  6.5 237.9 %copy-start = (bf16[1280,256]{1,0:T(8,128)(2,1)S(1)}, bf16[1280,256]{1,0:T(8,128)(2,1)}, u32[]{:S(2)}) copy-start(bf16[1280,256]{1,0:T(8,128)(2,1)} %param.16) | copy-start | bytes 1966084
  6.5 30.2 %copy-start.9 = (bf16[3,1280,160]{1,2,0:T(8,128)(2,1)S(1)}, bf16[3,1280,160]{1,2,0:T(8,128)(2,1)}, u32[]{:S(2)}) copy-start(bf16[3,1280,160]{1,2,0:T(8,128)(2,1)} %param.14) | copy-start | bytes 3686404
  6.5 95.9 %all-gather.4.cloned.1.call-start = ((), (), s32[]{:S(2)}) async-start(), calls=%async_computation | async-start | bytes 2703360 | tf_op jit(solution)/shard_map/all_gather | solution.py:76
  36.6 123.8 %all-gather.6.cloned.1.call-start = ((), (), s32[]{:S(2)}) async-start(), calls=%async_computation.1 | async-start | bytes 2703360 | tf_op jit(solution)/shard_map/all_gather | solution.py:77
  37.7 206.7 %all-reduce.2.cloned.1.call-start = ((), (), s32[]{:S(2)}) async-start(), calls=%async_computation.2 | async-start | bytes 1310720 | tf_op jit(solution)/shard_map/psum | solution.py:101
  108.0 5.7 %copy-start.1 = (f32[2,256,8192]{2,1,0:T(8,128)}, f32[2,256,8192]{2,1,0:T(8,128)S(1)}, u32[]{:S(2)}) copy-start(f32[2,256,8192]{2,1,0:T(8,128)S(1)} %get-tuple-element.6) | copy-start | bytes 50331652
  160.4 8.6 %copy-start.3 = (bf16[160,1280]{1,0:T(8,128)(2,1)S(1)}, bf16[160,1280]{1,0:T(8,128)(2,1)}, u32[]{:S(2)}) copy-start(bf16[160,1280]{1,0:T(8,128)(2,1)} %param.15) | copy-start | bytes 1228804
  168.9 77.1 %copy-start.6 = (f32[128]{0:T(128)S(1)}, f32[128]{0:T(128)}, u32[]{:S(2)}) copy-start(f32[128]{0:T(128)} %param.17) | copy-start | bytes 1540
  168.9 77.9 %copy-start.2 = (bf16[128,8192]{1,0:T(8,128)(2,1)S(1)}, bf16[128,8192]{1,0:T(8,128)(2,1)}, u32[]{:S(2)}) copy-start(bf16[128,8192]{1,0:T(8,128)(2,1)} %param.18) | copy-start | bytes 6291460
  168.9 78.4 %copy-start.10 = (f32[8192]{0:T(1024)S(1)}, f32[8192]{0:T(1024)}, u32[]{:S(2)}) copy-start(f32[8192]{0:T(1024)} %param.19) | copy-start | bytes 98308
  170.2 144.7 %all-gather.8.cloned.1.call-start = ((), (), s32[]{:S(2)}) async-start(), calls=%async_computation.3 | async-start | bytes 4325376 | tf_op jit(solution)/shard_map/all_gather | solution.py:116
  247.3 5.8 %copy-start.7 = (f32[128]{0:T(128)S(1)}, f32[128]{0:T(128)}, u32[]{:S(2)}) copy-start(f32[128]{0:T(128)} %param.21) | copy-start | bytes 1540
  247.3 5.8 %copy-start.4 = (s32[128]{0:T(128)S(1)}, s32[128]{0:T(128)}, u32[]{:S(2)}) copy-start(s32[128]{0:T(128)} %param.23) | copy-start | bytes 1540
  247.4 5.8 %copy-start.5 = (s32[128]{0:T(128)S(1)}, s32[128]{0:T(128)}, u32[]{:S(2)}) copy-start(s32[128]{0:T(128)} %param.22) | copy-start | bytes 1540
  315.1 10.6 %copy-start.8 = (bf16[8192,256]{0,1:T(8,128)(2,1)S(1)}, bf16[8192,256]{0,1:T(8,128)(2,1)}, u32[]{:S(2)}) copy-start(bf16[8192,256]{0,1:T(8,128)(2,1)} %all-gather.8.cloned.1.call-done) | copy-start | bytes 12582916
Sparse Core Ops, SparseCore 0:
  36.8 65.6 all-gather.3
  104.9 55.4 all-gather.5
  170.3 74.0 all-reduce.1
  246.9 67.8 all-gather.7
where the time goes:
time: 341 us; the launch traced here: 340 us
  waiting for transfers between devices  238 us (70%)
  matrix products  43.6 us (13%)
  blocking collectives  26.6 us (8%)
  between operations  13.4 us (4%)
  other arithmetic  11.9 us (3%)
  local copies, waits for them, and re-layouts  6.82 us (2%)
    psum x1, waiting for transfers between devices, on_device(): lax.psum(jnp.dot(attended, enc_out, preferred_element_type=jnp.float32).a...  74 us
    all_gather x1, waiting for transfers between devices, on_device(): key_shard = lax.all_gather(key_part, ('group', 'seq'), axis=0, tiled=True)  62.9 us
    all_gather x1, waiting for transfers between devices, on_device(): every_slab = lax.all_gather(kv_slab, ('group', 'seq'), axis=0, tiled=True)  58.9 us
    all_gather x1, waiting for transfers between devices, on_device(): lax.all_gather(value_part, ('group', 'seq'), axis=0, tiled=True)  41.9 us
    all_gather x1, blocking collectives, on_device(): gathered = lax.all_gather(patches, 'tensor', axis=0, tiled=True)  26.6 us
    dot_general x1, matrix products, on_device(): jnp.einsum('rgqd,kgd->gqrk', queries, slab_view[:, :, 0], preferred_eleme...  10.6 us
    dot_general x1, matrix products, on_device(): jnp.einsum('hrk,khd->hrd', weights.astype(jnp.bfloat16), value_heads, pre...  8.5 us
    dot_general x1, matrix products, on_device(): jnp.einsum('gqrk,kgd->rgqd', weights.astype(jnp.bfloat16), slab_view[:, :...  7.39 us
  transfers between devices with their start and end apart: 4, of which 4 were waited for; matrix products, arithmetic and copies ran while one was open for 7% of the time, Pallas kernels for 0%

commit v1 on v0

--- a/solution.py
+++ b/solution.py
@@ -98,9 +98,12 @@
     final_max, final_sum, final_mix = folded
     attended = (final_mix / final_sum[..., None]).astype(jnp.bfloat16)
     attended = attended.transpose(1, 0, 2).reshape(row_count, local_width)
-    total_out = lax.psum(
-        jnp.dot(attended, enc_out, preferred_element_type=jnp.float32).astype(jnp.bfloat16),
-        "tensor",
+    total_out = jnp.sum(
+        lax.all_gather(
+            jnp.dot(attended, enc_out, preferred_element_type=jnp.float32).astype(jnp.bfloat16),
+            "tensor",
+        ),
+        axis=0,
     ).astype(jnp.float32)
     encoded = (gathered.astype(jnp.float32) + total_out).astype(jnp.bfloat16)
     kv_local = cross_kv.shape[1] // (2 * HD)

time: 341 us -> 375 us (1.100)
  waiting for transfers between devices: 238 us -> 269 us
  other arithmetic: 11.9 us -> 17.1 us
    all_gather x0 -> x1, waiting for transfers between devices: none -> 109 us  [on_device(): lax.all_gather(jnp.dot(attended, enc_out, preferred_element_type=jnp.floa...]
    psum x1 -> x0, waiting for transfers between devices: 74 us -> none  [on_device(): lax.psum(jnp.dot(attended, enc_out, preferred_element_type=jnp.float32).a...]
    all_gather x1, waiting for transfers between devices: 58.9 us -> 54.5 us  [on_device(): every_slab = lax.all_gather(kv_slab, ('group', 'seq'), axis=0, tiled=True)]
  transfers between devices with their start and end apart: 4 -> 4, of which waited for: 4 -> 4; matrix products, arithmetic and copies ran while one was open for 7% -> 6% of each run, Pallas kernels for 0% -> 0%
where the time goes in v1:
time: 375 us; the launch traced here: 374 us
  waiting for transfers between devices  269 us (72%)
  matrix products  41.5 us (11%)
  blocking collectives  26.6 us (7%)
  other arithmetic  17.1 us (5%)
  between operations  13.4 us (4%)
  local copies, waits for them, and re-layouts  6.81 us (2%)
    all_gather x1, waiting for transfers between devices, on_device(): lax.all_gather(jnp.dot(attended, enc_out, preferred_element_type=jnp.floa...  109 us
    all_gather x1, waiting for transfers between devices, on_device(): key_shard = lax.all_gather(key_part, ('group', 'seq'), axis=0, tiled=True)  62.9 us
    all_gather x1, waiting for transfers between devices, on_device(): every_slab = lax.all_gather(kv_slab, ('group', 'seq'), axis=0, tiled=True)  54.5 us
    all_gather x1, waiting for transfers between devices, on_device(): lax.all_gather(value_part, ('group', 'seq'), axis=0, tiled=True)  41.9 us
    all_gather x1, blocking collectives, on_device(): gathered = lax.all_gather(patches, 'tensor', axis=0, tiled=True)  26.6 us
    dot_general x1, matrix products, on_device(): jnp.einsum('rgqd,kgd->gqrk', queries, slab_view[:, :, 0], preferred_eleme...  9.56 us
    dot_general x1, matrix products, on_device(): jnp.einsum('hrk,khd->hrd', weights.astype(jnp.bfloat16), value_heads, pre...  8.5 us
  transfers between devices with their start and end apart: 4, of which 4 were waited for; matrix products, arithmetic and copies ran while one was open for 6% of the time, Pallas kernels for 0%

profile of v1, /device:TPU:1, one launch (start us, length us, event | category | flops | bytes accessed | tf_op | source)
XLA Modules:
  0.0 374.4 jit_solution(8979524236819842896)
XLA Ops:
  6.5 26.6 %all_gather.18 = bf16[256,1280]{1,0:T(8,128)(2,1)S(1)} all-gather(bf16[32,1280]{1,0:T(8,128)(2,1)} %param.12), channel_id=1, replica_groups=mesh['group'=8,'tensor'=8,'seq'=4] {'tensor'}, dimensions={0}, use_global_device_ids=true | all-gather | bytes 737280 | tf_op jit(solution)/shard_map/all_gather | solution.py:43
  33.6 1.0 fusion.24
  34.6 2.0 convolution_convert_fusion.2
  36.7 1.0 convolution_convert_fusion.1
  37.9 0.4 convolution_convert_fusion.3
  38.3 1.2 broadcast_compare_fusion
  39.5 62.9 %all-gather.6.cloned.1.call-done = bf16[8192,160]{0,1:T(8,128)(2,1)} async-done(((bf16[256,160]{0,1:T(8,128)(2,1)}), bf16[8192,160]{0,1:T(8,128)(2,1)}) %all-gather.6.cloned.1.call-update) | async-done | bytes 2621456 | tf_op jit(solution)/shard_map/all_gather | solution.py:76
  102.4 5.6 %select_reduce_fusion = (f32[2,256]{1,0:T(2,128)S(1)}, f32[2,256,8192]{2,1,0:T(8,128)S(1)}) fusion(pred[256,8192]{1,0:T(8,128)(4,1)S(1)} %broadcast_compare_fusion, bf16[256,2,80]{0,2,1:T(8,128)(2,1)S(1)} %bitcast.130, bf16[8192,2,80]{0,2,1:T(8,128)(2,1)} %bitcast.128), kind=kOutput, calls=%fused_computation.2 | convolution fusion | flops 683671040 | bytes 21579776 | tf_op jit(solution)/shard_map/rhd,khd->hrk/dot_general | solution.py:84
  108.0 5.7 %copy-done.2 = f32[2,256,8192]{2,1,0:T(8,128)} copy-done((f32[2,256,8192]{2,1,0:T(8,128)}, f32[2,256,8192]{2,1,0:T(8,128)S(1)}, u32[]{:S(2)}) %copy-start.2) | copy-done | bytes 16777240
  113.7 4.8 %fusion.2 = f32[2,256]{1,0:T(2,128)S(1)} fusion(f32[2,256,8192]{2,1,0:T(8,128)S(1)} %get-tuple-element.6, f32[2,256]{1,0:T(2,128)S(1)} %broadcast_maximum_fusion, pred[256,8192]{1,0:T(8,128)(4,1)S(1)} %broadcast_compare_fusion), kind=kLoop, calls=%fused_computation.5 | loop fusion | flops 16776704 | bytes 18878464 | tf_op jit(solution)/shard_map/reduce_sum | solution.py:90
  118.5 41.9 %all-gather.8.cloned.1.call-done = bf16[8192,160]{0,1:T(8,128)(2,1)} async-done(((bf16[256,160]{0,1:T(8,128)(2,1)}), bf16[8192,160]{0,1:T(8,128)(2,1)}) %all-gather.8.cloned.1.call-update) | async-done | bytes 2621456 | tf_op jit(solution)/shard_map/all_gather | solution.py:77
  160.4 8.5 %fusion.35 = bf16[256,2,80]{0,2,1:T(8,128)(2,1)S(1)} fusion(bf16[8192,2,80]{0,2,1:T(8,128)(2,1)} %bitcast.129, f32[2,256,8192]{2,1,0:T(8,128)} %copy-done.2, f32[2,256]{1,0:T(2,128)S(1)} %broadcast_maximum_fusion, pred[256,8192]{1,0:T(8,128)(4,1)S(1)} %broadcast_compare_fusion, f32[256,2]{0,1:T(2,128)S(1)} %bitcast.125), kind=kOutput, calls=%fused_computation.42 | convolution fusion | flops 687947776 | bytes 21581824 | tf_op jit(solution)/shard_map/hrk,khd->hrd/dot_general | solution.py:91
  168.9 1.2 convolution_convert_fusion
  170.4 109.4 %all-gather.12.cloned.1.call-done = bf16[2048,1280]{1,0:T(8,128)(2,1)} async-done(((bf16[256,1280]{1,0:T(8,128)(2,1)}), bf16[2048,1280]{1,0:T(8,128)(2,1)}) %all-gather.12.cloned.1.call-update) | async-done | bytes 5242896 | tf_op jit(solution)/shard_map/all_gather | solution.py:102
  279.8 3.6 reduce_sum.80
  283.4 0.5 fusion.44
  284.0 0.7 pad_maximum_fusion
  284.7 2.1 fusion.12
  286.8 5.3 %fusion.100 = (f32[128,512]{1,0:T(8,128)S(1)}, f32[128,512]{1,0:T(8,128)S(1)}) fusion(bf16[8192,512]{1,0:T(8,128)(2,1)} %param.20, bf16[128,8192]{1,0:T(8,128)(2,1)} %param.18, f32[8192]{0:T(1024)S(1)} %copy-done.10, f32[128]{0:T(128)S(1)} %add_rsqrt_fusion.3), kind=kOutput, calls=%fused_computation.160 | convolution fusion | flops 1078001664 | bytes 11043328 | tf_op jit(solution)/shard_map/dot_general | solution.py:124
  292.6 2.8 compare_and_fusion
  295.4 54.5 %all-gather.10.cloned.1.call-done = bf16[8192,256]{0,1:T(8,128)(2,1)} async-done(((bf16[256,256]{0,1:T(8,128)(2,1)}), bf16[8192,256]{0,1:T(8,128)(2,1)}) %all-gather.10.cloned.1.call-update) | async-done | bytes 4194320 | tf_op jit(solution)/shard_map/all_gather | solution.py:119
  350.1 9.6 %fusion = (f32[4,128]{1,0:T(4,128)S(1)}, f32[8192,128,4]{1,0,2:T(8,128)}) fusion(pred[128,8192]{0,1:T(8,128)(4,1)S(1)} %compare_and_fusion, bf16[8192,1,2,128]{0,3,2,1:T(8,128)(2,1)} %bitcast.126, f32[128,512]{1,0:T(8,128)S(1)} %get-tuple-element.8, f32[16,8,4,128]{3,2,1,0:T(4,128)S(1)} %bitcast.122, f32[512]{0:T(512)S(1)} %broadcast_bitcast_fusion), kind=kOutput, calls=%fused_computation.3 | convolution fusion | flops 1082392064 | bytes 20451328 | tf_op jit(solution)/shard_map/rgqd,kgd->gqrk/dot_general | solution.py:137
  359.7 7.5 %fusion.41 = bf16[128,1,4,128]{0,3,2,1:T(8,128)(2,1)S(1)} fusion(f32[8192,128,4]{1,0,2:T(8,128)} %get-tuple-element.10, pred[128,8192]{0,1:T(8,128)(4,1)S(1)} %compare_and_fusion, bf16[8192,1,2,128]{0,3,2,1:T(8,128)(2,1)S(1)} %bitcast.127, f32[128,4]{0,1:T(4,128)S(1)} %bitcast.131), kind=kOutput, calls=%fused_computation.44 | convolution fusion | flops 1082261504 | bytes 20056064 | tf_op jit(solution)/shard_map/gqrk,kgd->rgqd/dot_general | solution.py:142
  367.1 0.8 copy.31
  (47 shorter events, 1.7 us)
Async XLA Ops:
  6.5 276.8 %copy-start = (bf16[1280,256]{1,0:T(8,128)(2,1)S(1)}, bf16[1280,256]{1,0:T(8,128)(2,1)}, u32[]{:S(2)}) copy-start(bf16[1280,256]{1,0:T(8,128)(2,1)} %param.16) | copy-start | bytes 1966084
  6.5 30.2 %copy-start.9 = (bf16[3,1280,160]{1,2,0:T(8,128)(2,1)S(1)}, bf16[3,1280,160]{1,2,0:T(8,128)(2,1)}, u32[]{:S(2)}) copy-start(bf16[3,1280,160]{1,2,0:T(8,128)(2,1)} %param.14) | copy-start | bytes 3686404
  6.5 95.9 %all-gather.6.cloned.1.call-start = ((), (), s32[]{:S(2)}) async-start(), calls=%async_computation | async-start | bytes 2703360 | tf_op jit(solution)/shard_map/all_gather | solution.py:76
  36.6 123.8 %all-gather.8.cloned.1.call-start = ((), (), s32[]{:S(2)}) async-start(), calls=%async_computation.1 | async-start | bytes 2703360 | tf_op jit(solution)/shard_map/all_gather | solution.py:77
  37.7 242.1 %all-gather.12.cloned.1.call-start = ((), (), s32[]{:S(2)}) async-start(), calls=%async_computation.3 | async-start | bytes 5898240 | tf_op jit(solution)/shard_map/all_gather | solution.py:102
  108.0 5.7 %copy-start.2 = (f32[2,256,8192]{2,1,0:T(8,128)}, f32[2,256,8192]{2,1,0:T(8,128)S(1)}, u32[]{:S(2)}) copy-start(f32[2,256,8192]{2,1,0:T(8,128)S(1)} %get-tuple-element.6) | copy-start | bytes 50331652
  160.4 8.5 %copy-start.3 = (bf16[160,1280]{1,0:T(8,128)(2,1)S(1)}, bf16[160,1280]{1,0:T(8,128)(2,1)}, u32[]{:S(2)}) copy-start(bf16[160,1280]{1,0:T(8,128)(2,1)} %param.15) | copy-start | bytes 1228804
  170.2 179.7 %all-gather.10.cloned.1.call-start = ((), (), s32[]{:S(2)}) async-start(), calls=%async_computation.2 | async-start | bytes 4325376 | tf_op jit(solution)/shard_map/all_gather | solution.py:119
  279.8 4.1 %copy-start.6 = (f32[128]{0:T(128)S(1)}, f32[128]{0:T(128)}, u32[]{:S(2)}) copy-start(f32[128]{0:T(128)} %param.17) | copy-start | bytes 1540
  279.8 7.0 %copy-start.10 = (f32[8192]{0:T(1024)S(1)}, f32[8192]{0:T(1024)}, u32[]{:S(2)}) copy-start(f32[8192]{0:T(1024)} %param.19) | copy-start | bytes 98308
  286.8 5.8 %copy-start.7 = (f32[128]{0:T(128)S(1)}, f32[128]{0:T(128)}, u32[]{:S(2)}) copy-start(f32[128]{0:T(128)} %param.21) | copy-start | bytes 1540
  286.8 5.8 %copy-start.4 = (s32[128]{0:T(128)S(1)}, s32[128]{0:T(128)}, u32[]{:S(2)}) copy-start(s32[128]{0:T(128)} %param.23) | copy-start | bytes 1540
  286.8 5.8 %copy-start.5 = (s32[128]{0:T(128)S(1)}, s32[128]{0:T(128)}, u32[]{:S(2)}) copy-start(s32[128]{0:T(128)} %param.22) | copy-start | bytes 1540
  350.1 9.6 %copy-start.8 = (bf16[8192,256]{0,1:T(8,128)(2,1)S(1)}, bf16[8192,256]{0,1:T(8,128)(2,1)}, u32[]{:S(2)}) copy-start(bf16[8192,256]{0,1:T(8,128)(2,1)} %all-gather.10.cloned.1.call-done) | copy-start | bytes 12582916
  359.7 8.2 %copy-start.1 = (bf16[1280,256]{1,0:T(8,128)(2,1)S(1)}, bf16[1280,256]{1,0:T(8,128)(2,1)}, u32[]{:S(2)}) copy-start(bf16[1280,256]{1,0:T(8,128)(2,1)} %param.16) | copy-start | bytes 1966084
Sparse Core Ops, SparseCore 0:
  36.8 65.6 all-gather.5
  104.9 55.4 all-gather.7
  170.3 109.4 all-gather.11
  284.8 65.0 all-gather.9
